TPU v7x, 256 devices: a whole 4x4x8 slice. The times are simulated.
256 devices in a mesh: grp: 8 (over z), slab: 32 (over y, x, core).
Axes of the slice: x: 4, y: 4, z: 8, core: 2. Of those that a mesh axis runs over, the one named last changes fastest.
Arguments:
- spectra: bfloat16 [131072, 2048], P(('grp', 'slab')), may hold values from -6 to 6
- ctf_sq: bfloat16 [131072, 1024], P(('grp', 'slab')), may hold values from 0.049804688 to 1
- dest: int32 [131072, 1], P(('grp', 'slab')), may hold values from 0 to 31; in each aligned block of 512 rows (0 to 511, 512 to 1023, ...) at most 32 rows name the same one
- block: int32 [131072], P(('grp', 'slab')), may hold values from 0 to 63
- pattern: int32 [131072], P(('grp', 'slab')), may hold values from 0 to 63
- pattern_table: bfloat16 [64, 8], replicated, may hold values from 0.049804688 to 1
- tau: float32 [1024], replicated, may hold values from 0.5 to 4
Outputs:
- image: float32 [2, 16, 1024, 1024], P(None, 'grp', None, 'slab')
Inputs may be any that keep to these rules, and one draw needn't show every extreme that they name: `dest`: among the rows of one device at most 32 name the same slab; in some device's rows one slab is named by exactly 32.
All inputs are finite; a program needn't handle non-finite values.
Results may differ from a plain program's by a relative error of at most 0.0003.
Values may be sent and summed in bfloat16 or wider, within the bound.
A program may use at most 192 MiB of HBM per device.

v0:
```python
import math

import jax
import jax.numpy as jnp
from jax import lax
from jax.sharding import PartitionSpec as P

KZ_DEV = 32
YWIN = 16
NBLK = 64


def dft_tables(length):
    indices = jnp.arange(length, dtype=jnp.int32)
    product = indices[:, None] * indices[None, :] % length
    angles = product.astype(jnp.float32) * (2.0 * math.pi / length)
    return (jnp.cos(angles), jnp.sin(angles))


def inverse_kz(filtered, cosine, sine):
    real_part = filtered[:, :, 0, :]
    imag_part = filtered[:, :, 1, :]
    scaling = 1.0 / math.sqrt(cosine.shape[0])
    highest = lax.Precision.HIGHEST
    out_real = jnp.einsum("zk,ykx->yzx", cosine, real_part, precision=highest) - jnp.einsum(
        "zk,ykx->yzx", sine, imag_part, precision=highest
    )
    out_imag = jnp.einsum("zk,ykx->yzx", sine, real_part, precision=highest) + jnp.einsum(
        "zk,ykx->yzx", cosine, imag_part, precision=highest
    )
    return jnp.stack([out_real * scaling, out_imag * scaling])


def on_device(spectra, ctf_sq, dest, block, pattern, pattern_table, tau):
    slab_count = lax.axis_size("slab")
    rows_here = spectra.shape[0]
    kx_width = ctf_sq.shape[1]
    spread = pattern_table.shape[1]
    capacity = max(2, 2 * rows_here // slab_count)
    slot_total = slab_count * capacity
    slab_ids = jnp.arange(slab_count, dtype=jnp.int32)
    matches = (dest == slab_ids[None, :]).astype(jnp.int32)
    earlier = jnp.cumsum(matches, axis=0) - matches
    position = jnp.sum(earlier * matches, axis=1)
    target = dest[:, 0] * capacity + position
    pattern_ids = jnp.arange(pattern_table.shape[0], dtype=jnp.int32)
    pattern_onehot = (pattern[:, None] == pattern_ids[None, :]).astype(jnp.bfloat16)
    row_weights = jnp.dot(pattern_onehot, pattern_table, preferred_element_type=jnp.float32).astype(
        jnp.bfloat16
    )
    block_label = (block + 1).astype(jnp.float32).astype(jnp.bfloat16)[:, None]
    send_spec = jnp.zeros((slot_total, 2 * kx_width), jnp.bfloat16).at[target].set(spectra)
    send_ctf = jnp.zeros((slot_total, kx_width), jnp.bfloat16).at[target].set(ctf_sq)
    send_weights = jnp.zeros((slot_total, spread), jnp.bfloat16).at[target].set(row_weights)
    send_label = jnp.zeros((slot_total, 1), jnp.bfloat16).at[target].set(block_label)
    got_spec, got_ctf, got_weights, got_label = (
        lax.all_to_all(send_spec, "slab", split_axis=0, concat_axis=0, tiled=True),
        lax.all_to_all(send_ctf, "slab", split_axis=0, concat_axis=0, tiled=True),
        lax.all_to_all(send_weights, "slab", split_axis=0, concat_axis=0, tiled=True),
        lax.all_to_all(send_label, "slab", split_axis=0, concat_axis=0, tiled=True),
    )
    block_ids = jnp.arange(1, NBLK + 1, dtype=jnp.int32).astype(jnp.float32)
    block_match = (got_label.astype(jnp.float32) == block_ids[None, :]).astype(jnp.bfloat16)
    spreader = (block_match[:, :, None] * got_weights[:, None, :]).reshape(
        slot_total, NBLK * spread
    )
    contract = (((0,), (0,)), ((), ()))
    cosine, sine = dft_tables(KZ_DEV * slab_count)
    column_width = kx_width // slab_count
    data_sum = lax.dot_general(spreader, got_spec, contract, preferred_element_type=jnp.float32)
    weight_sum = lax.dot_general(spreader, got_ctf, contract, preferred_element_type=jnp.float32)
    data_sum = data_sum.reshape(YWIN, KZ_DEV, 2, kx_width)
    weight_sum = weight_sum.reshape(YWIN, KZ_DEV, 1, kx_width)
    volume = jnp.concatenate([data_sum, weight_sum], axis=2)
    columns_all = lax.all_to_all(volume, "slab", split_axis=3, concat_axis=1, tiled=True)
    summed = lax.psum_scatter(columns_all, "grp", scatter_dimension=0, tiled=True)
    tau_part = lax.dynamic_slice_in_dim(tau, lax.axis_index("slab") * column_width, column_width, 0)
    filtered = summed[:, :, 0:2, :] / (summed[:, :, 2:3, :] + tau_part[None, None, None, :])
    image = inverse_kz(filtered, cosine, sine)
    return image


def solution(mesh):
    in_specs = (
        P(("grp", "slab"), None),
        P(("grp", "slab"), None),
        P(("grp", "slab"), None),
        P(("grp", "slab")),
        P(("grp", "slab")),
        P(),
        P(),
    )
    out_specs = P(None, "grp", None, "slab")
    return jax.shard_map(
        on_device, mesh=mesh, in_specs=in_specs, out_specs=out_specs, check_vma=False
    )
```

profile of v0, /device:TPU:1, one launch (start us, length us, event | category | flops | bytes accessed | tf_op | source)
XLA Modules:
  0.0 599.7 jit_solution(15534419843716490866)
XLA Ops:
  6.5 0.7 fusion.49
  7.2 1.2 reduce-window.6
  8.4 0.2 slice_reduce_fusion
  8.7 0.8 fusion.48
  9.4 0.7 compare_select_fusion
  10.1 0.7 convert_convert_fusion
  10.8 3.8 scatter_custom_fusion
  14.6 0.7 all_to_all.55
  15.3 8.6 %all-to-all-start = ((bf16[32,32,1]{1,2,0:T(2,128)(2,1)}), bf16[32,32,1]{1,2,0:T(2,128)(2,1)S(1)}, u32[]{:S(2)}, u32[]{:S(2)}) async-start(bf16[32,32,1]{1,2,0:T(2,128)(2,1)} %all_to_all.55), calls=%async_computation | async-start | bytes 32768 | tf_op jit(solution)/shard_map/all_to_all | solution.py:60
  23.9 0.9 convolution_convert_fusion
  24.8 0.2 copy.31
  25.0 1.8 scatter_custom_fusion.1
  26.8 0.1 copy.32
  27.0 0.7 reshape.148
  27.7 3.1 all-to-all-done
  30.8 4.2 all-to-all-start.1
  35.1 4.8 scatter_custom_fusion.3
  39.9 2.1 all-to-all-done.1
  42.0 5.7 all-to-all-start.3
  47.7 7.3 %scatter_custom_fusion.2 = bf16[1024,2048]{1,0:T(8,128)(2,1)} fusion(s32[512]{0:T(512)S(1)} %bitcast.129, bf16[512,2048]{1,0:T(8,128)(2,1)} %param.7, bf16[]{:T(256)} %constant.12.clone.1), kind=kCustom, calls=%fused_computation.24 | custom fusion | bytes 4194816 | tf_op jit(solution)/shard_map/scatter | solution.py:52
  55.0 21.3 %all-to-all-done.3 = bf16[32,32,1024]{2,1,0:T(8,128)(2,1)S(1)} async-done(((bf16[32,32,1024]{2,1,0:T(8,128)(2,1)}), bf16[32,32,1024]{2,1,0:T(8,128)(2,1)S(1)}, u32[]{:S(2)}, u32[]{:S(2)}) %all-to-all-start.3) | async-done | bytes 2097184 | tf_op jit(solution)/shard_map/all_to_all | solution.py:58
  76.2 6.1 %all-to-all-start.2 = ((bf16[32,32,2048]{2,1,0:T(8,128)(2,1)}), bf16[32,32,2048]{2,1,0:T(8,128)(2,1)}, u32[]{:S(2)}, u32[]{:S(2)}) async-start(bf16[32,32,2048]{2,1,0:T(8,128)(2,1)} %bitcast.115), calls=%async_computation.2 | async-start | bytes 8388608 | tf_op jit(solution)/shard_map/all_to_all | solution.py:57
  82.5 0.1 compare_convert_fusion
  82.7 0.1 mul.91
  82.9 0.1 broadcast_multiply_fusion
  83.0 2.7 convolution_bitcast_fusion
  85.7 47.4 %all-to-all-done.2 = bf16[32,32,2048]{2,1,0:T(8,128)(2,1)} async-done(((bf16[32,32,2048]{2,1,0:T(8,128)(2,1)}), bf16[32,32,2048]{2,1,0:T(8,128)(2,1)}, u32[]{:S(2)}, u32[]{:S(2)}) %all-to-all-start.2) | async-done | bytes 4194336 | tf_op jit(solution)/shard_map/all_to_all | solution.py:57
  133.0 6.4 %copy.34 = bf16[2048,1024]{1,0:T(8,128)(2,1)} copy(bf16[2048,1024]{0,1:T(8,128)(2,1)} %bitcast.13) | data formatting | bytes 8388608 | tf_op jit(solution)/shard_map/dot_general | solution.py:70
  139.4 4.7 fusion.68
  144.1 3.3 pad_maximum_fusion
  147.4 18.1 %copy.35 = f32[16,32,3,1024]{1,0,2,3:T(8,128)} copy(f32[16,32,3,1024]{3,1,2,0:T(8,128)} %pad_maximum_fusion) | data formatting | bytes 12582912 | tf_op jit(solution)/shard_map/concatenate | solution.py:74
  165.5 27.1 %reshape.150 = f32[32,1,49152]{2,1,0:T(1,128)} reshape(f32[1024,3,16,32]{3,2,1,0:T(8,128)} %bitcast.114) | data formatting | bytes 12582912
  192.7 82.1 %all_to_all.61 = f32[32,1,49152]{2,1,0:T(1,128)} all-to-all(f32[32,1,49152]{2,1,0:T(1,128)} %reshape.150), channel_id=1, replica_groups=mesh['grp'=8,'slab'=32] {'slab'}, dimensions={0} | all-to-all | bytes 12582912 | tf_op jit(solution)/shard_map/all_to_all | solution.py:75
  274.8 0.5 broadcast.112
  275.3 19.9 %reduce.6 = f32[32,49152]{1,0:T(8,128)} reduce(f32[32,1,49152]{2,1,0:T(1,128)} %all_to_all.61, f32[]{:T(128)} %broadcast.112), dimensions={1}, to_apply=%all_to_all.51.reduce_sub_computation | reduce | bytes 12582916 | tf_op jit(solution)/shard_map/all_to_all | solution.py:75
  295.2 24.4 %reshape.151 = f32[1024,3,16,32]{3,2,1,0:T(8,128)} reshape(f32[32,49152]{1,0:T(8,128)} %reduce.6) | data formatting | bytes 12582912
  319.6 24.7 %copy.36 = f32[16,32,32,3,32]{2,1,4,0,3:T(8,128)} copy(f32[16,32,32,3,32]{2,0,3,4,1:T(8,128)} %bitcast.113) | data formatting | bytes 12582912 | tf_op jit(solution)/shard_map/all_to_all | solution.py:75
  344.3 20.1 %all_to_all.54 = f32[16,1024,3,32]{1,3,0,2:T(8,128)} reshape(f32[16,32,32,3,32]{2,1,4,0,3:T(8,128)} %copy.36) | data formatting | bytes 12582912 | tf_op jit(solution)/shard_map/all_to_all | solution.py:75
  364.4 0.8 dynamic_slice.3
  365.2 0.6 dynamic-slice
  366.4 146.4 %all-reduce.3.cloned.1.call-done = f32[16,1024,3,32]{1,3,0,2:T(8,128)} async-done(((f32[16,1024,3,32]{1,3,0,2:T(8,128)}), f32[16,1024,3,32]{1,3,0,2:T(8,128)}) %all-reduce.3.cloned.1.call-update) | async-done | bytes 6291472
  512.8 1.0 fusion.42
  513.9 1.1 dynamic-slice_divide_fusion
  515.0 19.1 %fusion.5 = f32[2,32,1024]{2,1,0:T(8,128)S(1)} fusion(f32[2,1024,2,32]{1,3,0,2:T(8,128)S(1)} %dynamic-slice_divide_fusion), kind=kOutput, calls=%fused_computation.13 | convolution fusion | flops 819986432 | bytes 524288 | tf_op jit(solution)/shard_map/zk,ykx->yzx/dot_general | solution.py:25
  534.1 19.4 %fusion.3 = f32[2,32,1024]{2,1,0:T(8,128)S(1)} fusion(f32[2,1024,2,32]{1,3,0,2:T(8,128)S(1)} %dynamic-slice_divide_fusion), kind=kOutput, calls=%fused_computation.11 | convolution fusion | flops 819986432 | bytes 524288 | tf_op jit(solution)/shard_map/zk,ykx->yzx/dot_general | solution.py:28
  553.5 19.0 %fusion.37 = f32[1,2,1024,32]{2,3,1,0:T(8,128)S(1)} fusion(f32[2,32,1024]{2,1,0:T(8,128)S(1)} %fusion.5, f32[2,1024,2,32]{1,3,0,2:T(8,128)S(1)} %dynamic-slice_divide_fusion), kind=kOutput, calls=%fused_computation.32 | convolution fusion | flops 820117504 | bytes 786432 | tf_op jit(solution)/shard_map/zk,ykx->yzx/dot_general | solution.py:25
  572.5 19.3 %fusion.31 = f32[1,2,1024,32]{2,3,1,0:T(8,128)S(1)} fusion(f32[2,32,1024]{2,1,0:T(8,128)S(1)} %fusion.3, f32[2,1024,2,32]{1,3,0,2:T(8,128)S(1)} %dynamic-slice_divide_fusion), kind=kOutput, calls=%fused_computation.30 | convolution fusion | flops 820117504 | bytes 786432 | tf_op jit(solution)/shard_map/zk,ykx->yzx/dot_general | solution.py:28
  591.8 0.8 pad_maximum_fusion.1
  (17 shorter events, 0.3 us)
Async XLA Ops:
  6.5 17.3 %copy-start = (bf16[64,8]{0,1:T(8,128)(2,1)S(1)}, bf16[64,8]{0,1:T(8,128)(2,1)}, u32[]{:S(2)}) copy-start(bf16[64,8]{0,1:T(8,128)(2,1)} %param.12) | copy-start | bytes 3076
  15.3 15.6 %all-to-all-start = ((bf16[32,32,1]{1,2,0:T(2,128)(2,1)}), bf16[32,32,1]{1,2,0:T(2,128)(2,1)S(1)}, u32[]{:S(2)}, u32[]{:S(2)}) async-start(bf16[32,32,1]{1,2,0:T(2,128)(2,1)} %all_to_all.55), calls=%async_computation | async-start | bytes 32768 | tf_op jit(solution)/shard_map/all_to_all | solution.py:60
  30.8 11.1 %all-to-all-start.1 = ((bf16[32,2,128]{2,1,0:T(2,128)(2,1)}), bf16[32,2,128]{2,1,0:T(2,128)(2,1)S(1)}, u32[]{:S(2)}, u32[]{:S(2)}) async-start(bf16[32,2,128]{2,1,0:T(2,128)(2,1)} %reshape.148), calls=%async_computation.1 | async-start | bytes 32768 | tf_op jit(solution)/shard_map/all_to_all | solution.py:59
  42.0 34.3 %all-to-all-start.3 = ((bf16[32,32,1024]{2,1,0:T(8,128)(2,1)}), bf16[32,32,1024]{2,1,0:T(8,128)(2,1)S(1)}, u32[]{:S(2)}, u32[]{:S(2)}) async-start(bf16[32,32,1024]{2,1,0:T(8,128)(2,1)} %bitcast.18), calls=%async_computation.3 | async-start | bytes 4194304 | tf_op jit(solution)/shard_map/all_to_all | solution.py:58
  76.2 56.8 %all-to-all-start.2 = ((bf16[32,32,2048]{2,1,0:T(8,128)(2,1)}), bf16[32,32,2048]{2,1,0:T(8,128)(2,1)}, u32[]{:S(2)}, u32[]{:S(2)}) async-start(bf16[32,32,2048]{2,1,0:T(8,128)(2,1)} %bitcast.115), calls=%async_computation.2 | async-start | bytes 8388608 | tf_op jit(solution)/shard_map/all_to_all | solution.py:57
  82.3 430.5 %all-reduce.3.cloned.1.call-start = ((), (), s32[]{:S(2)}) async-start(), calls=%async_computation.5 | async-start | bytes 12582912
  139.4 4.7 copy-start.2
  364.4 0.8 copy-start.3
  572.5 20.2 %copy-start.1 = (bf16[64,8]{0,1:T(8,128)(2,1)S(1)}, bf16[64,8]{0,1:T(8,128)(2,1)}, u32[]{:S(2)}) copy-start(bf16[64,8]{0,1:T(8,128)(2,1)} %param.12) | copy-start | bytes 3076
Sparse Core Ops, SparseCore 0:
  364.5 148.2 all-reduce.2
where the time goes:
time: 609 us; the launch traced here: 600 us
  waiting for transfers between devices  220 us (36%)
  local copies, waits for them, and re-layouts  143 us (23%)
  matrix products  85.1 us (14%)
  blocking collectives  82.1 us (13%)
  other arithmetic  30.5 us (5%)
  starting transfers between devices  24.7 us (4%)
  between operations  14.4 us (2%)
    unnamed x2, waiting for transfers between devices  146 us
    all_to_all x1, blocking collectives, on_device(): lax.all_to_all(volume, 'slab', split_axis=3, concat_axis=1, tiled=True)  82.1 us
    unnamed x13, local copies, waits for them, and re-layouts  52.9 us
    all_to_all x1, waiting for transfers between devices, on_device(): lax.all_to_all(send_spec, 'slab', split_axis=0, concat_axis=0, tiled=True)  47.4 us
    all_to_all x3, local copies, waits for them, and re-layouts, on_device(): lax.all_to_all(volume, 'slab', split_axis=3, concat_axis=1, tiled=True)  45.3 us
    all_to_all x1, waiting for transfers between devices, on_device(): lax.all_to_all(send_ctf, 'slab', split_axis=0, concat_axis=0, tiled=True)  21.3 us
    all_to_all x1, other arithmetic, on_device(): lax.all_to_all(volume, 'slab', split_axis=3, concat_axis=1, tiled=True)  19.9 us
    dot_general x1, matrix products, inverse_kz(): jnp.einsum('zk,ykx->yzx', sine, real_part, precision=highest)  19.4 us
  transfers between devices with their start and end apart: 5, of which 5 were waited for; matrix products, arithmetic and copies ran while one was open for 3% of the time, Pallas kernels for 0%

commit v1 on v0

v1 whole, which is shorter than its diff:
```python
import functools
import math

import jax
import jax.numpy as jnp
import numpy as np
from jax import lax
from jax.experimental import pallas as pl
from jax.experimental.pallas import tpu as pltpu
from jax.sharding import PartitionSpec as P

MESH = pl.DeviceIdType.MESH
BF = jnp.bfloat16
F32 = jnp.float32
NS = 32
NG = 8
ROWS = 512
COLS = 96
NT = (((1,), (1,)), ((), ()))


def whole(n):
    return [pl.BlockSpec(memory_space=pltpu.VMEM)] * n


def pack_kernel(spec, ctf, dcol, drow, blk, pat, eye, xt, meta):
    me = lax.axis_index("slab")
    for chunk in range(12):
        plane, first = chunk // 4, chunk % 4
        src = spec[:, chunk * 256 : chunk * 256 + 256] if plane < 2 else ctf[:, first * 256 : first * 256 + 256]
        part = lax.dot_general(eye[...], src, NT, preferred_element_type=F32).astype(BF)
        for i in range(8):
            xt[first * 8 + i, plane * 32 : plane * 32 + 32, :] = part[i * 32 : i * 32 + 32, :]
    later = lax.broadcasted_iota(jnp.int32, (ROWS, ROWS), 0) < lax.broadcasted_iota(jnp.int32, (ROWS, ROWS), 1)
    same = (dcol[...] == drow[...]) & later
    pos = jnp.sum(jnp.where(same, 1.0, 0.0), axis=0, keepdims=True)
    d = drow[...]
    slot = (128 * (d >> 2) + 32 * ((d + me) & 3)).astype(F32) + pos
    code = (blk[...] * 64 + pat[...]).astype(F32)
    for t in range(4):
        meta[t : t + 1, :] = slot[:, t * 128 : t * 128 + 128]
        meta[4 + t : 5 + t, :] = code[:, t * 128 : t * 128 + 128]


def exchange_kernel(xt, meta, got, gotm, own, ownm, lsem, ssem, rsem, smsem, rmsem):
    me = lax.axis_index("slab")
    first = pltpu.make_async_copy(xt.at[me], own, lsem.at[0])
    firstm = pltpu.make_async_copy(meta, ownm, lsem.at[1])
    first.start()
    firstm.start()
    barrier = pltpu.get_barrier_semaphore()
    for t in range(1, NS):
        pl.semaphore_signal(barrier, inc=1, device_id={"slab": lax.rem(me + t, NS)}, device_id_type=MESH)
    pl.semaphore_wait(barrier, NS - 1)

    def copies(t):
        peer = lax.rem(me + t, NS)
        source = lax.rem(me + NS - t, NS)
        small = pltpu.make_async_remote_copy(
            meta, gotm.at[me], smsem.at[t], rmsem.at[t], device_id={"slab": peer}, device_id_type=MESH
        )
        big = pltpu.make_async_remote_copy(
            xt.at[peer], got.at[me], ssem.at[t], rsem.at[t], device_id={"slab": peer}, device_id_type=MESH
        )
        del source
        return small, big

    sent = [copies(t) for t in range(1, NS)]
    for small, big in sent:
        small.start()
        big.start()
    first.wait()
    firstm.wait()
    last = pltpu.make_async_copy(own, got.at[me], lsem.at[0])
    lastm = pltpu.make_async_copy(ownm, gotm.at[me], lsem.at[1])
    last.start()
    lastm.start()
    last.wait()
    lastm.wait()
    for small, big in sent:
        small.wait()
        big.wait()


def spread_kernel(got, gotm, table, iota, groups, vol, xa, pt, y, xs, st, vt):
    def pick(parts):
        lane = groups[0 : parts[0].shape[0], :] if parts[0].dtype == BF else groups[0 : parts[0].shape[0], :].astype(F32)
        return jnp.where(lane < 1.0, parts[0], jnp.where(lane < 2.0, parts[1], jnp.where(lane < 3.0, parts[2], parts[3])))

    sub = lax.broadcasted_iota(jnp.int32, (16, 128), 0)
    half = jnp.where(sub >= 8, 1.0, 0.0)

    @pl.loop(0, NS // 4)
    def _(quad):
        for jj in range(4):
            j = quad * 4 + jj
            m = gotm[j]
            xa[0:COLS, :] = got[j]
            slots = []
            for t in range(4):
                code = m[4 + t : 5 + t, :]
                blk = jnp.floor(code * (1.0 / 64.0))
                pat = code - blk * 64.0
                patb = jnp.broadcast_to(pat, (64, 128)).astype(BF)
                hot = jnp.where(patb == iota[0:64, :], 1.0, 0.0).astype(BF)
                w = jnp.dot(table[...], hot, preferred_element_type=F32)
                xa[COLS : COLS + 16, t * 128 : t * 128 + 128] = w.astype(BF)
                xa[COLS + 16 : COLS + 32, t * 128 : t * 128 + 128] = (jnp.broadcast_to(blk, (16, 128)) - half).astype(BF)
                slots.append(jnp.broadcast_to(m[t : t + 1, :], (16, 128)))
            for n in range(4):
                for t in range(4):
                    v = (slots[t] - 256.0 * n).astype(BF)
                    for g in range(16):
                        pt[g * 16 : g * 16 + 16, t * 128 : t * 128 + 128] = jnp.where(
                            v == iota[g * 16 : g * 16 + 16, :], jnp.ones_like(v), jnp.zeros_like(v)
                        )
                y[jj, :, n * 256 : n * 256 + 256] = lax.dot_general(
                    xa[...], pt[...], NT, preferred_element_type=F32
                ).astype(BF)
        lanes = pl.ds(pl.multiple_of(quad * 128, 128), 128)
        for q in range(8):
            tiles = [y[jj, :, q * 128 : q * 128 + 128] for jj in range(4)]
            for s in range(4):
                xs[q * 4 + s, :, lanes] = pick([tiles[(g - s) % 4] for g in range(4)])

    @pl.loop(0, NS // 4)
    def _(q):
        for s in range(4):
            slab = q * 4 + s
            w16 = xs[slab, COLS : COLS + 16, :]
            lab = xs[slab, COLS + 16 : COLS + 32, :]
            for i in range(32):
                u, g, b = i // 8, (i // 2) % 4, i % 2
                base = 4 * (4 * u + (g - s) % 4) + 2 * b
                st[i * 16 : i * 16 + 16, :] = jnp.where(lab == jnp.full_like(lab, base), w16, jnp.zeros_like(w16))
            for h in range(2):
                vt[s, :, h * 256 : h * 256 + 256] = lax.dot_general(
                    xs[slab, 0:COLS, :], st[h * 256 : h * 256 + 256, :], NT, preferred_element_type=F32
                )
        for u in range(4):
            tiles = [vt[s, :, u * 128 : u * 128 + 128] for s in range(4)]
            for a in range(4):
                vol[2 * u + a // 2, (a % 2) * 8 + q] = pick([tiles[(g - a) % 4] for g in range(4)])


PARTS = 4
TILES = 16 // PARTS


def reduce_kernel(v, out, local, ra, rb, lsem, sa, ka, sb, kb):
    me = lax.axis_index("grp")
    loads = []
    for i in range(NG):
        o = lax.rem(me + i, NG)
        load = pltpu.make_async_copy(v.at[o], local.at[o], lsem.at[i])
        load.start()
        loads.append(load)
    barrier = pltpu.get_barrier_semaphore()
    for step in (1, NG - 1):
        pl.semaphore_signal(barrier, inc=1, device_id={"grp": lax.rem(me + step, NG)}, device_id_type=MESH)
    pl.semaphore_wait(barrier, 2)
    for load in loads:
        load.wait()

    chains = []
    for p in range(PARTS):
        sign = 1 if p % 2 == 0 else -1
        chains.append((p, sign, 4, ra, sa, ka))
        chains.append((p, -sign, 3, rb, sb, kb))
    copies = {}

    def chunk(p, sign, hops):
        return local.at[lax.rem(me + sign * hops + NG, NG), pl.ds(p * TILES, TILES)]

    for t in range(1, 5):
        for c, (p, sign, length, buf, ssem, rsem) in enumerate(chains):
            if t > length:
                continue
            mine = chunk(p, sign, length - t + 1)
            if t == 1:
                src = mine
            else:
                copies[c, t - 1].wait_recv()
                src = buf.at[p, t - 2]
                src[...] += mine[...]
            copy = pltpu.make_async_remote_copy(
                src,
                buf.at[p, t - 1],
                ssem.at[p, t - 1],
                rsem.at[p, t - 1],
                device_id={"grp": lax.rem(me + sign + NG, NG)},
                device_id_type=MESH,
            )
            copy.start()
            copies[c, t] = copy
    for p in range(PARTS):
        copies[2 * p + 1, 3].wait_recv()
        copies[2 * p, 4].wait_recv()
        out[p * TILES : p * TILES + TILES] = local[me, p * TILES : p * TILES + TILES] + ra[p, 3] + rb[p, 2]
    for copy in copies.values():
        copy.wait_send()


def image_kernel(u, tau, are, aim, bre, bim, out, wh, wl, lhs):
    g = lax.axis_index("grp")

    @pl.loop(0, NS)
    def _(s):
        xr, xi = are[pl.ds(s, 1), :], aim[pl.ds(s, 1), :]
        rows = pl.ds(pl.multiple_of(s * 32, 32), 32)
        for part in range(2):
            w = bre[...] * xr - bim[...] * xi if part == 0 else bre[...] * xi + bim[...] * xr
            hi = w.astype(BF)
            wh[rows, part * 1024 : part * 1024 + 1024] = hi
            wl[rows, part * 1024 : part * 1024 + 1024] = (w - hi.astype(F32)).astype(BF)

    for y in range(2):
        shift = lax.rem(128 - 32 * (2 * (g & 1) + y), 128)
        for q in range(8):
            tile = u[y * 8 + q]
            scale = tile[64:96] + tau[...]
            for part in range(2):
                f = pltpu.roll(tile[part * 32 : part * 32 + 32] / scale, shift, 1)
                hi = f.astype(BF)
                r = part * 64 + y * 32
                lhs[r : r + 32, q * 128 : q * 128 + 128] = hi
                lhs[128 + r : 160 + r, q * 128 : q * 128 + 128] = (f - hi.astype(F32)).astype(BF)

    def product(first):
        cols = pl.ds(first, 256)
        full = jnp.dot(lhs[...], wh[:, cols], preferred_element_type=F32)
        return full[0:128] + full[128:256] + jnp.dot(lhs[0:128, :], wl[:, cols], preferred_element_type=F32)

    for n in range(4):
        c = product(n * 256)
        s = product(1024 + n * 256)
        out[0, :, n * 256 : n * 256 + 256] = c[0:64] - s[64:128]
        out[1, :, n * 256 : n * 256 + 256] = s[0:64] + c[64:128]


def factors():
    z = np.arange(1024)
    digit = np.arange(32)[:, None]
    coarse = 2.0 * math.pi * (32 * digit * z % 1024) / 1024
    fine = 2.0 * math.pi * (digit * z % 1024) / 1024
    scale = 1.0 / 32.0
    return [np.asarray(a, np.float32) for a in (np.cos(coarse), np.sin(coarse), scale * np.cos(fine), scale * np.sin(fine))]


def params(**more):
    return pltpu.CompilerParams(vmem_limit_bytes=60 * 1024 * 1024, **more)


def shape(dims, dtype):
    return jax.ShapeDtypeStruct(dims, dtype)


ANY = pl.BlockSpec(memory_space=pl.ANY)


def pack(spectra, ctf_sq, dest, block, pattern):
    eye = jnp.eye(256, dtype=BF)
    return pl.pallas_call(
        pack_kernel,
        out_shape=(shape((NS, COLS, ROWS), BF), shape((8, 128), F32)),
        in_specs=whole(7),
        out_specs=tuple(whole(2)),
        compiler_params=params(),
        name="pack",
    )(spectra, ctf_sq, dest, dest.reshape(1, ROWS), block.reshape(1, ROWS), pattern.reshape(1, ROWS), eye)


def exchange(xt, meta):
    dma = pltpu.SemaphoreType.DMA
    return pl.pallas_call(
        exchange_kernel,
        out_shape=(shape((NS, COLS, ROWS), BF), shape((NS, 8, 128), F32)),
        in_specs=[ANY] * 2,
        out_specs=(ANY, ANY),
        scratch_shapes=[
            pltpu.VMEM((COLS, ROWS), BF),
            pltpu.VMEM((8, 128), F32),
            dma((2,)),
            dma((NS,)),
            dma((NS,)),
            dma((NS,)),
            dma((NS,)),
        ],
        compiler_params=pltpu.CompilerParams(collective_id=0, has_side_effects=True),
        name="exchange",
    )(xt, meta)


def spread(got, gotm, pattern_table):
    iota = jnp.asarray(np.tile(np.arange(256)[:, None], (1, 128)), BF)
    groups = jnp.asarray(np.tile(np.arange(128)[None, :] // 32, (128, 1)), BF)
    table = jnp.concatenate([pattern_table.T, pattern_table.T], axis=0)
    return pl.pallas_call(
        spread_kernel,
        out_shape=shape((NG, 16, COLS, 128), F32),
        in_specs=whole(5),
        out_specs=whole(1)[0],
        scratch_shapes=[
            pltpu.VMEM((128, ROWS), BF),
            pltpu.VMEM((256, ROWS), BF),
            pltpu.VMEM((4, 128, 1024), BF),
            pltpu.VMEM((NS, 128, 1024), BF),
            pltpu.VMEM((512, 1024), BF),
            pltpu.VMEM((4, COLS, 512), F32),
        ],
        compiler_params=params(),
        name="spread",
    )(got, gotm, table, iota, groups)


def reduce_ring(vol):
    dma = pltpu.SemaphoreType.DMA
    return pl.pallas_call(
        reduce_kernel,
        out_shape=shape((16, COLS, 128), F32),
        in_specs=[ANY],
        out_specs=whole(1)[0],
        scratch_shapes=[
            pltpu.VMEM((NG, 16, COLS, 128), F32),
            pltpu.VMEM((PARTS, 4, TILES, COLS, 128), F32),
            pltpu.VMEM((PARTS, 3, TILES, COLS, 128), F32),
            dma((NG,)),
            dma((PARTS, 4)),
            dma((PARTS, 4)),
            dma((PARTS, 3)),
            dma((PARTS, 3)),
        ],
        compiler_params=params(collective_id=1, has_side_effects=True),
        name="reduce",
    )(vol)


def image_of(summed, tau):
    s = lax.axis_index("slab")
    column = lax.dynamic_slice_in_dim(tau, s * 32, 32, 0).reshape(32, 1)
    return pl.pallas_call(
        image_kernel,
        out_shape=shape((2, 64, 1024), F32),
        in_specs=whole(6),
        out_specs=whole(1)[0],
        scratch_shapes=[pltpu.VMEM((1024, 2048), BF), pltpu.VMEM((1024, 2048), BF), pltpu.VMEM((256, 1024), BF)],
        compiler_params=params(),
        name="image",
    )(summed, column, *[jnp.asarray(a) for a in factors()])


def on_device(spectra, ctf_sq, dest, block, pattern, pattern_table, tau):
    xt, meta = pack(spectra, ctf_sq, dest, block, pattern)
    got, gotm = exchange(xt, meta)
    vol = spread(got, gotm, pattern_table)
    summed = reduce_ring(vol)
    image = image_of(summed, tau)
    return jnp.transpose(image.reshape(2, 2, 32, 1024), (0, 1, 3, 2))


def solution(mesh):
    rows = P(("grp", "slab"))
    wide = P(("grp", "slab"), None)
    return jax.shard_map(
        on_device,
        mesh=mesh,
        in_specs=(wide, wide, wide, rows, rows, P(), P()),
        out_specs=P(None, "grp", None, "slab"),
        check_vma=False,
    )
```

time: 609 us -> 180 us (0.30); the launches traced: 600 us -> 180 us
  waiting for transfers between devices: 220 us -> 0 us
  Pallas kernels: 0 us -> 176 us
  local copies, waits for them, and re-layouts: 143 us -> 2.32 us
  matrix products: 85.1 us -> 0 us
  blocking collectives: 82.1 us -> 0 us
  other arithmetic: 30.5 us -> 1.26 us
  starting transfers between devices: 24.7 us -> 0 us
  between operations: 14.4 us -> 0.04 us
    pallas_call x0 -> x5, Pallas kernels: none -> 176 us  [the longest x1 69.1 us: reduce_ring(): pl.pallas_call(reduce_kernel, out_shape=shape((16, COLS, 128), F32), in_s...]
    unnamed x2 -> x0, waiting for transfers between devices: 146 us -> none
    dot_general x7 -> x0, matrix products: 85.1 us -> none  [the longest x1 19.4 us: inverse_kz(): jnp.einsum('zk,ykx->yzx', sine, real_part, precision=highest)]
    all_to_all x1 -> x0, blocking collectives: 82.1 us -> none  [on_device(): lax.all_to_all(volume, 'slab', split_axis=3, concat_axis=1, tiled=True)]
    all_to_all x4 -> x0, waiting for transfers between devices: 73.9 us -> none  [the longest x1 47.4 us: on_device(): lax.all_to_all(send_spec, 'slab', split_axis=0, concat_axis=0, tiled=True)]
    unnamed x13 -> x5, local copies, waits for them, and re-layouts: 52.9 us -> 1.55 us
    all_to_all x6 -> x0, local copies, waits for them, and re-layouts: 46.1 us -> none  [the longest x3 45.3 us: on_device(): lax.all_to_all(volume, 'slab', split_axis=3, concat_axis=1, tiled=True)]
    all_to_all x4 -> x0, starting transfers between devices: 24.6 us -> none  [the longest x1 8.58 us: on_device(): lax.all_to_all(send_label, 'slab', split_axis=0, concat_axis=0, tiled=True)]
  transfers between devices with their start and end apart: 5 -> 0, of which waited for: 5 -> 0; matrix products, arithmetic and copies ran while one was open for 3% -> 0% of each run, Pallas kernels for 0% -> 0%
where the time goes in v1:
time: 180 us
  Pallas kernels  176 us (98%)
  local copies, waits for them, and re-layouts  2.32 us (1%)
    pallas_call x1, Pallas kernels, reduce_ring(): pl.pallas_call(reduce_kernel, out_shape=shape((16, COLS, 128), F32), in_s...  69.1 us
    pallas_call x1, Pallas kernels, exchange(): pl.pallas_call(exchange_kernel, out_shape=(shape((NS, COLS, ROWS), BF), s...  60.6 us
    pallas_call x1, Pallas kernels, spread(): pl.pallas_call(spread_kernel, out_shape=shape((NG, 16, COLS, 128), F32),...  35.6 us
    pallas_call x1, Pallas kernels, image_of(): pl.pallas_call(image_kernel, out_shape=shape((2, 64, 1024), F32), in_spec...  6.39 us
    pallas_call x1, Pallas kernels, pack(): pl.pallas_call(pack_kernel, out_shape=(shape((NS, COLS, ROWS), BF), shape...  4.66 us

profile of v1, /device:TPU:1, one launch (start us, length us, event | category | flops | bytes accessed | tf_op | source)
XLA Modules:
  0.0 179.9 jit_solution(6396472952224860521)
XLA Ops:
  0.0 0.0 copy-start
  0.0 1.5 copy.14.dcol
  1.6 0.7 fusion.eye
  2.2 0.0 copy-start.1
  2.2 4.7 %pack.1 = (bf16[32,96,512]{2,1,0:T(8,128)(2,1)}, f32[8,128]{1,0:T(8,128)}) custom-call(bf16[512,2048]{1,0:T(8,128)(2,1)} %spec.1, bf16[512,1024]{1,0:T(8,128)(2,1)} %ctf.1, s32[512,1]{1,0:T(8,128)} %copy.14.dcol, s32[1,512]{1,0:T(1,128)} %bitcast.9, s32[1,512]{1,0:T(1,128)} %bitcast.10, s32[1,512]{1,0:T(1,128)} %bitcast.11, bf16[256,256]{1,0:T(8,128)(2,1)} %fusion.eye), custom_call_target="tpu_custom_call" | custom-call | tf_op jit(solution)/shard_map/pack/pallas_call | solution.py:263
  6.9 60.6 %exchange.1 = (bf16[32,96,512]{2,1,0:T(8,128)(2,1)}, f32[32,8,128]{2,1,0:T(8,128)}) custom-call(bf16[32,96,512]{2,1,0:T(8,128)(2,1)} %get-tuple-element.9.xt, f32[8,128]{1,0:T(8,128)} %get-tuple-element.10.meta), custom_call_target="tpu_custom_call" | custom-call | tf_op jit(solution)/shard_map/exchange/pallas_call | solution.py:275
  67.5 0.0 copy-done.1
  67.5 0.6 pad_maximum_fusion.table
  68.1 35.6 %spread.1.v = f32[8,16,96,128]{3,2,1,0:T(8,128)} custom-call(bf16[32,96,512]{2,1,0:T(8,128)(2,1)} %get-tuple-element.11.got, f32[32,8,128]{2,1,0:T(8,128)} %get-tuple-element.12.gotm, bf16[16,64]{1,0:T(8,128)(2,1)} %pad_maximum_fusion.table, bf16[256,128]{1,0:T(8,128)(2,1)} %constant.22.clone.iota, bf16[128,128]{1,0:T(8,128)(2,1)} %constant.23.clone.groups), custom_call_target="tpu_custom_call" | custom-call | tf_op jit(solution)/shard_map/spread/pallas_call | solution.py:298
  103.6 69.1 %reduce.1.u = f32[16,96,128]{2,1,0:T(8,128)} custom-call(f32[8,16,96,128]{3,2,1,0:T(8,128)} %spread.1.v), custom_call_target="tpu_custom_call" | custom-call | tf_op jit(solution)/shard_map/reduce/pallas_call | solution.py:318
  172.7 0.0 copy-done
  172.8 0.1 dynamic-slice_bitcast_fusion
  172.8 0.7 copy.15.tau
  173.5 6.4 %image.1 = f32[2,64,1024]{2,1,0:T(8,128)} custom-call(f32[16,96,128]{2,1,0:T(8,128)} %reduce.1.u, f32[32,1]{1,0:T(8,128)} %copy.15.tau, f32[32,1024]{1,0:T(8,128)} %constant.24.clone.are, f32[32,1024]{1,0:T(8,128)} %constant.25.clone.aim, f32[32,1024]{1,0:T(8,128)} %constant.26.clone.bre, f32[32,1024]{1,0:T(8,128)} %constant.27.clone.bim), custom_call_target="tpu_custom_call" | custom-call | tf_op jit(solution)/shard_map/image/pallas_call | solution.py:341
Async XLA Ops:
  0.0 172.7 %copy-start = (f32[1024]{0:T(1024)S(1)}, f32[1024]{0:T(1024)}, u32[]{:S(2)}) copy-start(f32[1024]{0:T(1024)} %param.19) | copy-start | bytes 12292
  2.2 65.2 %copy-start.1 = (bf16[64,8]{0,1:T(8,128)(2,1)S(1)}, bf16[64,8]{0,1:T(8,128)(2,1)}, u32[]{:S(2)}) copy-start(bf16[64,8]{0,1:T(8,128)(2,1)} %param.18) | copy-start | bytes 3076

commit v2 on v0

v2 whole, which is shorter than its diff:
```python
import math

import jax
import jax.numpy as jnp
import numpy as np
from jax import lax
from jax.experimental import pallas as pl
from jax.experimental.pallas import tpu as pltpu
from jax.sharding import PartitionSpec as P

MESH = pl.DeviceIdType.MESH
BF = jnp.bfloat16
F32 = jnp.float32
NS = 32
NG = 8
ROWS = 512
PIECES = 2
KX = 16
COLS = 3 * KX
NT = (((1,), (1,)), ((), ()))


def kernel(
    spec, ctf, drow, blk, pat, tau, eye, table, iota, groups, are, aim, bre, bim,
    out,
    xt0, xt1, got0, got1, meta, xa, pt, y, xs, st, vt, vol, ra, rb, wh, wl, lhs, taucol,
    ssem0, ssem1, rsem0, rsem1, sa, ka, sb, kb,
):
    me = lax.axis_index("slab")
    g = lax.axis_index("grp")
    quad0 = me // 4

    barrier = pltpu.get_barrier_semaphore()
    for t in range(1, NS):
        pl.semaphore_signal(barrier, inc=1, device_id={"slab": lax.rem(me + t, NS)}, device_id_type=MESH)
    for step in (1, NG - 1):
        pl.semaphore_signal(barrier, inc=1, device_id={"grp": lax.rem(g + step, NG)}, device_id_type=MESH)

    d = drow[...]
    dtile = [d[:, t * 128 : t * 128 + 128].astype(F32) for t in range(4)]
    dcol = [jnp.transpose(jnp.broadcast_to(v, (128, 128))) for v in dtile]
    before = lax.broadcasted_iota(jnp.int32, (128, 128), 0) < lax.broadcasted_iota(jnp.int32, (128, 128), 1)
    for t in range(4):
        pos = jnp.zeros((1, 128), F32)
        for r in range(t + 1):
            same = dcol[r] == jnp.broadcast_to(dtile[t], (128, 128))
            if r == t:
                same = same & before
            pos = pos + jnp.sum(jnp.where(same, 1.0, 0.0), axis=0, keepdims=True)
        dt = d[:, t * 128 : t * 128 + 128]
        meta[t : t + 1, :] = (dt >> 2).astype(F32)
        meta[4 + t : 5 + t, :] = (32 * ((dt + me) & 3)).astype(F32) + pos
        meta[8 + t : 9 + t, :] = blk[:, t * 128 : t * 128 + 128].astype(F32)
        meta[12 + t : 13 + t, :] = pat[:, t * 128 : t * 128 + 128].astype(F32)
    metab = meta[...].astype(BF)

    for chunk in range(12):
        plane, first = chunk // 4, chunk % 4
        src = spec[:, chunk * 256 : chunk * 256 + 256] if plane < 2 else ctf[:, first * 256 : first * 256 + 256]
        part = lax.dot_general(eye[...], src, NT, preferred_element_type=F32).astype(BF)
        for i in range(8):
            for t in range(4):
                lanes = slice(t * 128, t * 128 + 128)
                xt0[first * 8 + i, plane * 4 + t] = part[i * 32 : i * 32 + 16, lanes]
                xt1[first * 8 + i, plane * 4 + t] = part[i * 32 + 16 : i * 32 + 32, lanes]
    for s in range(NS):
        xt0[s, 12] = metab

    pl.semaphore_wait(barrier, NS - 1 + 2)
    sends = []
    for xt, got, ssem, rsem in ((xt0, got0, ssem0, rsem0), (xt1, got1, ssem1, rsem1)):
        pltpu.make_async_copy(xt.at[me], got.at[me], rsem.at[me]).start()
        for i in range(8):
            for m in range(4):
                if i == 0 and m == 0:
                    continue
                peer = lax.rem(quad0 + 8 - i, 8) * 4 + lax.rem(me + m, 4)
                copy = pltpu.make_async_remote_copy(
                    xt.at[peer], got.at[me], ssem.at[i * 4 + m], rsem.at[me],
                    device_id={"slab": peer}, device_id_type=MESH,
                )
                copy.start()
                sends.append(copy)

    @pl.loop(0, NS)
    def _(s):
        xr, xi = are[pl.ds(s, 1), :], aim[pl.ds(s, 1), :]
        rows = pl.ds(pl.multiple_of(s * 32, 32), 32)
        for part in range(2):
            w = bre[...] * xr - bim[...] * xi if part == 0 else bre[...] * xi + bim[...] * xr
            hi = w.astype(BF)
            wh[rows, part * 1024 : part * 1024 + 1024] = hi
            wl[rows, part * 1024 : part * 1024 + 1024] = (w - hi.astype(F32)).astype(BF)

    taurow = tau[:, pl.ds(pl.multiple_of(quad0 * 128, 128), 128)]
    taucol[...] = jnp.transpose(jnp.broadcast_to(taurow, (128, 128)))

    def pick(parts):
        lane = groups[0 : parts[0].shape[0], :]
        lane = lane if parts[0].dtype == BF else lane.astype(F32)
        return jnp.where(lane < 1.0, parts[0], jnp.where(lane < 2.0, parts[1], jnp.where(lane < 3.0, parts[2], parts[3])))

    sub = lax.broadcasted_iota(jnp.int32, (16, 128), 0)
    half = jnp.where(sub >= 8, 1.0, 0.0)

    def place(piece, step):
        got, rsem = ((got0, rsem0), (got1, rsem1))[piece]
        quad = lax.rem(quad0 + step, 8)
        height = COLS + 32 if piece == 0 else COLS
        for jj in range(4):
            j = quad * 4 + jj
            pltpu.make_async_copy(got.at[j], got.at[j], rsem.at[j]).wait()
            m = got0[j, 12].astype(F32)
            for t in range(4):
                lanes = slice(t * 128, t * 128 + 128)
                for plane in range(3):
                    xa[plane * 16 : plane * 16 + 16, lanes] = got[j, plane * 4 + t]
                if piece == 0:
                    patb = jnp.broadcast_to(m[12 + t : 13 + t, :], (64, 128)).astype(BF)
                    hot = jnp.where(patb == iota[0:64, :], 1.0, 0.0).astype(BF)
                    w = jnp.dot(table[...], hot, preferred_element_type=F32)
                    xa[COLS : COLS + 16, lanes] = w.astype(BF)
                    xa[COLS + 16 : COLS + 32, lanes] = (jnp.broadcast_to(m[8 + t : 9 + t, :], (16, 128)) - half).astype(BF)
            slots = [jnp.broadcast_to(m[t : t + 1, :] * 128.0 + m[4 + t : 5 + t, :], (16, 128)) for t in range(4)]
            for n in range(4):
                for t in range(4):
                    v = (slots[t] - 256.0 * n).astype(BF)
                    for r in range(16):
                        pt[r * 16 : r * 16 + 16, t * 128 : t * 128 + 128] = jnp.where(
                            v == iota[r * 16 : r * 16 + 16, :], jnp.ones_like(v), jnp.zeros_like(v)
                        )
                y[jj, 0:height, n * 256 : n * 256 + 256] = lax.dot_general(
                    xa[0:height, :], pt[...], NT, preferred_element_type=F32
                ).astype(BF)
        lanes = pl.ds(pl.multiple_of(quad * 128, 128), 128)
        for q in range(8):
            tiles = [y[jj, 0:height, q * 128 : q * 128 + 128] for jj in range(4)]
            for s in range(4):
                xs[q * 4 + s, 0:height, lanes] = pick([tiles[(l - s) % 4] for l in range(4)])

    def spread(piece, u):
        base = jnp.full((16, 1024), (16 * u).astype(F32)).astype(BF)

        @pl.loop(0, 8)
        def _(q):
            for s in range(4):
                slab = q * 4 + s
                w16 = xs[slab, COLS : COLS + 16, :]
                lab = xs[slab, COLS + 16 : COLS + 32, :] - base
                for i in range(8):
                    mine = 4 * ((i // 2 - s) % 4) + 2 * (i % 2)
                    st[s, i * 16 : i * 16 + 16, :] = jnp.where(lab == jnp.full_like(lab, mine), w16, jnp.zeros_like(w16))
                vt[s] = lax.dot_general(xs[slab, 0:COLS, :], st[s], NT, preferred_element_type=F32)
            tiles = [vt[s] for s in range(4)]
            for a in range(4):
                vol[piece, 2 * u + a // 2, (a % 2) * 8 + q] = pick([tiles[(l - a) % 4] for l in range(4)])

    ring = {}

    def hop(piece, chain, t):
        buf, ssem, rsem = ((ra, sa, ka), (rb, sb, kb))[chain]
        for part in range(2):
            sign = (1 if part == 0 else -1) * (1 if chain == 0 else -1)
            owner = lax.rem(g + sign * (4 - chain - t + 1) + NG, NG)
            mine = vol.at[piece, owner, pl.ds(part * 8, 8)]
            if t == 1:
                src = mine
            else:
                ring[piece, chain, t - 1, part].wait_recv()
                src = buf.at[piece, part, t - 2]
                src[...] += mine[...]
            copy = pltpu.make_async_remote_copy(
                src, buf.at[piece, part, t - 1], ssem.at[piece, part, t - 1], rsem.at[piece, part, t - 1],
                device_id={"grp": lax.rem(g + sign + NG, NG)}, device_id_type=MESH,
            )
            copy.start()
            ring[piece, chain, t, part] = copy

    def image(piece):
        for part in range(2):
            ring[piece, 1, 3, part].wait_recv()
            ring[piece, 0, 4, part].wait_recv()
        lam = taucol[pl.ds(pl.multiple_of(lax.rem(me, 4) * 32 + piece * KX, 16), KX), :]
        for part in range(2):
            shift = lax.rem(128 - 32 * (2 * (g & 1) + part), 128)
            for q in range(8):
                tile = vol[piece, g, part * 8 + q] + ra[piece, part, 3, q] + rb[piece, part, 2, q]
                scale = tile[2 * KX : 3 * KX] + lam
                for c in range(2):
                    f = pltpu.roll(tile[c * KX : c * KX + KX] / scale, shift, 1)
                    hi = f.astype(BF)
                    r = c * 32 + part * KX
                    lhs[r : r + KX, q * 128 : q * 128 + 128] = hi
                    lhs[64 + r : 64 + r + KX, q * 128 : q * 128 + 128] = (f - hi.astype(F32)).astype(BF)

        def product(first):
            cols = slice(first, first + 256)
            full = jnp.dot(lhs[...], wh[:, cols], preferred_element_type=F32)
            return full[0:64] + full[64:128] + jnp.dot(lhs[0:64, :], wl[:, cols], preferred_element_type=F32)

        for n in range(4):
            c = product(n * 256)
            s = product(1024 + n * 256)
            for part in range(2):
                rows = slice(part * 32 + piece * KX, part * 32 + piece * KX + KX)
                low, high = slice(part * KX, part * KX + KX), slice(32 + part * KX, 32 + part * KX + KX)
                out[0, rows, n * 256 : n * 256 + 256] = c[low] - s[high]
                out[1, rows, n * 256 : n * 256 + 256] = s[low] + c[high]

    far = lax.rem(g + 4, NG) // 2
    way = 1 - 2 * (g & 1)
    order = [far, lax.rem(far - way + 4, 4), lax.rem(far + way + 4, 4), g // 2]

    @pl.loop(0, 8)
    def _(step):
        place(0, step)

    spread(0, order[0])
    hop(0, 0, 1)
    spread(0, order[1])
    hop(0, 1, 1)
    spread(0, order[2])
    hop(0, 0, 2)
    spread(0, order[3])
    hop(0, 1, 2)

    def places(first, last):
        @pl.loop(first, last)
        def _(step):
            place(1, step)

    places(0, 2)
    hop(0, 0, 3)
    places(2, 4)
    hop(0, 1, 3)
    places(4, 6)
    hop(0, 0, 4)
    places(6, 8)
    spread(1, order[0])
    hop(1, 0, 1)
    spread(1, order[1])
    hop(1, 1, 1)
    spread(1, order[2])
    hop(1, 0, 2)
    spread(1, order[3])
    hop(1, 1, 2)
    hop(1, 0, 3)
    image(0)
    hop(1, 1, 3)
    hop(1, 0, 4)
    image(1)
    for copy in sends:
        copy.wait_send()
    for copy in ring.values():
        copy.wait_send()


def factors():
    z = np.arange(1024)
    digit = np.arange(32)[:, None]
    coarse = 2.0 * math.pi * (32 * digit * z % 1024) / 1024
    fine = 2.0 * math.pi * (digit * z % 1024) / 1024
    scale = 1.0 / 32.0
    return [np.asarray(a, np.float32) for a in (np.cos(coarse), np.sin(coarse), scale * np.cos(fine), scale * np.sin(fine))]


def on_device(spectra, ctf_sq, dest, block, pattern, pattern_table, tau):
    iota = jnp.asarray(np.tile(np.arange(256)[:, None], (1, 128)), BF)
    groups = jnp.asarray(np.tile(np.arange(128)[None, :] // 32, (128, 1)), BF)
    table = jnp.concatenate([pattern_table.T, pattern_table.T], axis=0)
    dma = pltpu.SemaphoreType.DMA
    operands = (
        spectra, ctf_sq, dest.reshape(1, ROWS), block.reshape(1, ROWS), pattern.reshape(1, ROWS), tau.reshape(1, 1024),
        jnp.eye(256, dtype=BF), table, iota, groups, *[jnp.asarray(a) for a in factors()],
    )
    image = pl.pallas_call(
        kernel,
        out_shape=jax.ShapeDtypeStruct((2, 64, 1024), F32),
        in_specs=[pl.BlockSpec(memory_space=pltpu.VMEM)] * len(operands),
        out_specs=pl.BlockSpec(memory_space=pltpu.VMEM),
        scratch_shapes=[
            pltpu.VMEM((NS, 13, 16, 128), BF),
            pltpu.VMEM((NS, 12, 16, 128), BF),
            pltpu.VMEM((NS, 13, 16, 128), BF),
            pltpu.VMEM((NS, 12, 16, 128), BF),
            pltpu.VMEM((16, 128), F32),
            pltpu.VMEM((COLS + 32, ROWS), BF),
            pltpu.VMEM((256, ROWS), BF),
            pltpu.VMEM((4, COLS + 32, 1024), BF),
            pltpu.VMEM((NS, COLS + 32, 1024), BF),
            pltpu.VMEM((4, 128, 1024), BF),
            pltpu.VMEM((4, COLS, 128), F32),
            pltpu.VMEM((PIECES, NG, 16, COLS, 128), F32),
            pltpu.VMEM((PIECES, 2, 4, 8, COLS, 128), F32),
            pltpu.VMEM((PIECES, 2, 3, 8, COLS, 128), F32),
            pltpu.VMEM((1024, 2048), BF),
            pltpu.VMEM((1024, 2048), BF),
            pltpu.VMEM((128, 1024), BF),
            pltpu.VMEM((128, 128), F32),
            dma((NS,)),
            dma((NS,)),
            dma((NS,)),
            dma((NS,)),
            dma((PIECES, 2, 4)),
            dma((PIECES, 2, 4)),
            dma((PIECES, 2, 3)),
            dma((PIECES, 2, 3)),
        ],
        compiler_params=pltpu.CompilerParams(
            collective_id=0, has_side_effects=True, vmem_limit_bytes=62 * 1024 * 1024
        ),
        name="backproject",
    )(*operands)
    return jnp.transpose(image.reshape(2, 2, 32, 1024), (0, 1, 3, 2))


def solution(mesh):
    rows = P(("grp", "slab"))
    wide = P(("grp", "slab"), None)
    return jax.shard_map(
        on_device,
        mesh=mesh,
        in_specs=(wide, wide, wide, rows, rows, P(), P()),
        out_specs=P(None, "grp", None, "slab"),
        check_vma=False,
    )
```

time: 609 us -> 122 us (0.20)
  the two profiles are of different devices: /device:TPU:1 before, /device:TPU:29 now
where the time goes in v2:
time: 122 us
  Pallas kernels  118 us (97%)
  other arithmetic  2.03 us (2%)
  local copies, waits for them, and re-layouts  1.89 us (2%)
    pallas_call x1, Pallas kernels, on_device(): pl.pallas_call(kernel, out_shape=jax.ShapeDtypeStruct((2, 64, 1024), F32)...  118 us

profile of v2, /device:TPU:29, one launch (start us, length us, event | category | flops | bytes accessed | tf_op | source)
XLA Modules:
  0.0 122.0 jit_solution(10495814986763675637)
XLA Ops:
  0.0 1.4 %pad_maximum_fusion.table = bf16[16,64]{1,0:T(8,128)(2,1)} fusion(bf16[8,64]{1,0:T(8,128)(2,1)} %bitcast.13), kind=kLoop, calls=%fused_computation.2 | loop fusion | flops 4096 | bytes 3072 | tf_op jit(solution)/shard_map/concatenate | solution.py:270
  1.4 0.7 fusion.eye
  2.0 118.1 %backproject.1 = f32[2,64,1024]{2,1,0:T(8,128)} custom-call(bf16[512,2048]{1,0:T(8,128)(2,1)} %spec.1, bf16[512,1024]{1,0:T(8,128)(2,1)} %ctf.1, s32[1,512]{1,0:T(1,128)} %bitcast.10, s32[1,512]{1,0:T(1,128)} %bitcast.11, s32[1,512]{1,0:T(1,128)} %bitcast.12, f32[1,1024]{1,0:T(1,128)} %bitcast.9, bf16[256,256]{1,0:T(8,128)(2,1)} %fusion.eye, ...), custom_call_target="tpu_custom_call" | custom-call | tf_op jit(solution)/shard_map/backproject/pallas_call | solution.py:276
  120.2 1.9 %copy.15 = f32[2,2,1024,32]{2,3,1,0:T(8,128)} copy(f32[2,2,1024,32]{2,3,1,0:T(8,128)} %bitcast.8) | data formatting | bytes 1048576

commit v3 on v2

v3 whole, which is shorter than its diff:
```python
import math

import jax
import jax.numpy as jnp
import numpy as np
from jax import lax
from jax.experimental import pallas as pl
from jax.experimental.pallas import tpu as pltpu
from jax.sharding import PartitionSpec as P

MESH = pl.DeviceIdType.MESH
BF = jnp.bfloat16
F32 = jnp.float32
NS = 32
NG = 8
ROWS = 512
PIECES = 2
KX = 16
SMALL = 11
COLS = 3 * KX
NT = (((1,), (1,)), ((), ()))


ROW_STEPS = (1, 3, 0, 2)


def steps_away(step):
    late, r = step // 4, step % 4
    t = (r + r // 2) % 2
    even, odd = 2 * (r % 2), 2 * (r % 2) + 1
    return (even, (1 - late) * (1 + 2 * t) + late * (2 - 2 * t)), (odd, (1 - late) * (3 - 2 * t) + late * 2 * t)


def kernel(
    spec, ctf, *rest,
):
    small_in, out = rest[:SMALL], rest[SMALL]
    raw, small = rest[SMALL + 1], rest[SMALL + 2 : 2 * SMALL + 2]
    (
        xt0, xt1, got0, got1, mrow, perm, meta, xa, pt, y, xs0, xs1, st, vt, vol, ra, rb, wh, wl, lhs, taucol,
        insem, smallsem, ssem0, ssem1, rsem0, rsem1, sa, ka, sb, kb,
    ) = rest[2 * SMALL + 2 :]
    drow, blk, pat, tau, iota, tab, groups, are, aim, bre, bim = small
    me = lax.axis_index("slab")
    g = lax.axis_index("grp")
    row, col, core = me // 8, (me // 2) % 4, me % 2

    barrier = pltpu.get_barrier_semaphore()
    for t in range(1, NS):
        pl.semaphore_signal(barrier, inc=1, device_id={"slab": lax.rem(me + t, NS)}, device_id_type=MESH)
    for step in (1, NG - 1):
        pl.semaphore_signal(barrier, inc=1, device_id={"grp": lax.rem(g + step, NG)}, device_id_type=MESH)

    loads = [pltpu.make_async_copy(a, b, smallsem.at[i]) for i, (a, b) in enumerate(zip(small_in, small))]
    for load in loads[:8]:
        load.start()
    fetches = []
    for i in range(4):
        first = lax.rem(row + 4 - ROW_STEPS[i], 4) * 256
        for plane in range(3):
            source, start = (spec, first + plane * 1024) if plane < 2 else (ctf, first)
            fetch = pltpu.make_async_copy(
                source.at[:, pl.ds(pl.multiple_of(start, 256), 256)], raw.at[i, plane], insem.at[i, plane]
            )
            fetch.start()
            fetches.append(fetch)
    for load in loads[8:]:
        load.start()
    for load in loads[:8]:
        load.wait()

    d = drow[...]
    dtile = [d[:, t * 128 : t * 128 + 128].astype(F32) for t in range(4)]
    dcol = [jnp.transpose(jnp.broadcast_to(v, (128, 128))) for v in dtile]
    before = lax.broadcasted_iota(jnp.int32, (128, 128), 0) < lax.broadcasted_iota(jnp.int32, (128, 128), 1)
    mrow[...] = jnp.zeros_like(mrow)
    for t in range(4):
        lanes = slice(t * 128, t * 128 + 128)
        pos = jnp.zeros((1, 128), F32)
        rank = jnp.zeros((1, 128), F32)
        wide = jnp.broadcast_to(dtile[t], (128, 128))
        for r in range(4):
            rank = rank + jnp.sum(jnp.where(dcol[r] < wide, 1.0, 0.0), axis=0, keepdims=True)
            if r <= t:
                same = dcol[r] == wide
                if r == t:
                    same = same & before
                pos = pos + jnp.sum(jnp.where(same, 1.0, 0.0), axis=0, keepdims=True)
        dt = d[:, lanes]
        mrow[0:1, lanes] = (dt >> 2).astype(F32)
        mrow[1:2, lanes] = (32 * ((dt + me) & 3)).astype(F32) + pos
        mrow[2:3, lanes] = blk[:, lanes].astype(F32)
        mrow[3:4, lanes] = pat[:, lanes].astype(F32)
        rank16 = jnp.broadcast_to(rank + pos, (16, 128))
        for n in range(2):
            v = (rank16 - 256.0 * n).astype(BF)
            for r in range(16):
                perm[n * 256 + r * 16 : n * 256 + r * 16 + 16, lanes] = jnp.where(
                    v == iota[r * 16 : r * 16 + 16, :], jnp.ones_like(v), jnp.zeros_like(v)
                )
    mrow[...] = lax.dot_general(mrow[...].astype(BF), perm[...], NT, preferred_element_type=F32)
    for v in range(4):
        for t in range(4):
            meta[v * 4 + t : v * 4 + t + 1, :] = mrow[v : v + 1, t * 128 : t * 128 + 128]
    metab = meta[...].astype(BF)

    sends = []

    def send(piece, step):
        xt, got, ssem, rsem = ((xt0, got0, ssem0, rsem0), (xt1, got1, ssem1, rsem1))[piece]
        for odd, (dx, dy) in enumerate(steps_away(step)):
            chip = lax.rem(row + 4 - dy, 4) * 4 + lax.rem(col + 4 - dx, 4)
            for m in range(2):
                if dx or dy or m:
                    copy = pltpu.make_async_remote_copy(
                        xt.at[chip * 2 + lax.rem(core + m, 2)], got.at[me], ssem.at[step * 4 + odd * 2 + m], rsem.at[me],
                        device_id={"slab": chip * 2 + lax.rem(core + m, 2)}, device_id_type=MESH,
                    )
                    copy.start()
                    sends.append(copy)

    for i in range(4):
        octet = lax.rem(row + 4 - ROW_STEPS[i], 4) * 8
        for plane in range(3):
            fetches[i * 3 + plane].wait()
            part = lax.dot_general(
                jnp.transpose(raw[i, plane]), perm[...], NT, preferred_element_type=F32
            ).astype(BF)
            for k in range(8):
                for t in range(4):
                    lanes = slice(t * 128, t * 128 + 128)
                    xt0[octet + k, plane * 4 + t] = part[k * 32 : k * 32 + 16, lanes]
                    xt1[octet + k, plane * 4 + t] = part[k * 32 + 16 : k * 32 + 32, lanes]
        for k in range(8):
            xt0[octet + k, 12] = metab
        if i == 1:
            pl.semaphore_wait(barrier, NS - 1 + 2)
            for step in range(4):
                send(0, step)
        if i == 2:
            pltpu.make_async_copy(xt0.at[me], got0.at[me], rsem0.at[me]).start()
            pltpu.make_async_copy(xt1.at[me], got1.at[me], rsem1.at[me]).start()
    for step in range(4, 8):
        send(0, step)
    tabf = tab[...].astype(F32)
    table = jnp.concatenate([tabf, tabf], axis=0).astype(BF)

    def tables():
        for load in loads[8:]:
            load.wait()

        @pl.loop(0, NS)
        def _(s):
            xr, xi = are[pl.ds(s, 1), :], aim[pl.ds(s, 1), :]
            rows = pl.ds(pl.multiple_of(s * 32, 32), 32)
            for part in range(2):
                w = bre[...] * xr - bim[...] * xi if part == 0 else bre[...] * xi + bim[...] * xr
                hi = w.astype(BF)
                wh[rows, part * 1024 : part * 1024 + 1024] = hi
                wl[rows, part * 1024 : part * 1024 + 1024] = (w - hi.astype(F32)).astype(BF)

        taurow = tau[:, pl.ds(pl.multiple_of(me // 4 * 128, 128), 128)]
        taucol[...] = jnp.transpose(jnp.broadcast_to(taurow, (128, 128)))

    def pick(parts):
        lane = groups[0 : parts[0].shape[0], :]
        lane = lane if parts[0].dtype == BF else lane.astype(F32)
        return jnp.where(lane < 1.0, parts[0], jnp.where(lane < 2.0, parts[1], jnp.where(lane < 3.0, parts[2], parts[3])))

    sub = lax.broadcasted_iota(jnp.int32, (16, 128), 0)
    half = jnp.where(sub >= 8, 1.0, 0.0)

    def place(piece, step):
        got, rsem = ((got0, rsem0), (got1, rsem1))[piece]
        even, odd = steps_away(step)
        height = COLS + 32 if piece == 0 else COLS
        for jj in range(4):
            same = 1 - lax.rem(col + jj // 2, 2)
            dx, dy = (same * e + (1 - same) * o for e, o in zip(even, odd))
            j = (lax.rem(row + dy, 4) * 4 + lax.rem(col + dx, 4)) * 2 + jj % 2
            pltpu.make_async_copy(got.at[j], got.at[j], rsem.at[j]).wait()
            m = got0[j, 12].astype(F32)
            for t in range(4):
                lanes = slice(t * 128, t * 128 + 128)
                for plane in range(3):
                    xa[plane * 16 : plane * 16 + 16, lanes] = got[j, plane * 4 + t]
                if piece == 0:
                    patb = jnp.broadcast_to(m[12 + t : 13 + t, :], (64, 128)).astype(BF)
                    hot = jnp.where(patb == iota[0:64, :], 1.0, 0.0).astype(BF)
                    w = jnp.dot(table, hot, preferred_element_type=F32)
                    xa[COLS : COLS + 16, lanes] = w.astype(BF)
                    xa[COLS + 16 : COLS + 32, lanes] = (jnp.broadcast_to(m[8 + t : 9 + t, :], (16, 128)) - half).astype(BF)
            slots = [jnp.broadcast_to(m[t : t + 1, :] * 128.0 + m[4 + t : 5 + t, :], (16, 128)) for t in range(4)]
            low, high = (0, 0, 0, 2), (2, 4, 4, 4)
            for n in range(4):
                band = slice(low[n] * 128, high[n] * 128)
                for t in range(low[n], high[n]):
                    v = (slots[t] - 256.0 * n).astype(BF)
                    for r in range(16):
                        pt[n % 2, r * 16 : r * 16 + 16, t * 128 : t * 128 + 128] = jnp.where(
                            v == iota[r * 16 : r * 16 + 16, :], jnp.ones_like(v), jnp.zeros_like(v)
                        )
                y[jj, 0:height, n * 256 : n * 256 + 256] = lax.dot_general(
                    xa[0:height, band], pt[n % 2, :, band], NT, preferred_element_type=F32
                ).astype(BF)
        xs = xs0 if piece == 0 else xs1
        lanes = pl.ds(pl.multiple_of(step * 128, 128), 128)
        for q in range(8):
            tiles = [y[jj, 0:height, q * 128 : q * 128 + 128] for jj in range(4)]
            for s in range(4):
                xs[q * 4 + s, 0:height, lanes] = pick([tiles[(l - s) % 4] for l in range(4)])

    def spread(piece, groups_of):
        width = 128 * len(groups_of)
        xs = xs0 if piece == 0 else xs1
        shifts = [[jnp.full((16, 1024), (8 * o).astype(F32)).astype(BF) for o in owners] for owners in groups_of]

        @pl.loop(0, 8)
        def _(q):
            for s in range(4):
                slab = q * 4 + s
                w16 = xs0[slab, COLS : COLS + 16, :]
                lab16 = xs0[slab, COLS + 16 : COLS + 32, :]
                for n, shift in enumerate(shifts):
                    lab = [lab16 - shift[0], lab16 - shift[1]]
                    for i in range(8):
                        a = (i // 2 - s) % 4
                        mine = 4 * (a % 2) + 2 * (i % 2)
                        st[s, n * 128 + i * 16 : n * 128 + i * 16 + 16, :] = jnp.where(
                            lab[a // 2] == jnp.full_like(w16, mine), w16, jnp.zeros_like(w16)
                        )
                vt[s, :, 0:width] = lax.dot_general(xs[slab, 0:COLS, :], st[s, 0:width, :], NT, preferred_element_type=F32)
            for n, owners in enumerate(groups_of):
                tiles = [vt[s, :, n * 128 : n * 128 + 128] for s in range(4)]
                for a in range(4):
                    vol[piece, owners[a // 2], (a % 2) * 8 + q] = pick([tiles[(l - a) % 4] for l in range(4)])

    ring = {}

    def hop(piece, chain, t, parts=(0, 1)):
        buf, ssem, rsem = ((ra, sa, ka), (rb, sb, kb))[chain]
        for part in parts:
            sign = (1 if part == 0 else -1) * (1 if chain == 0 else -1)
            owner = lax.rem(g + sign * (4 - chain - t + 1) + NG, NG)
            mine = vol.at[piece, owner, pl.ds(part * 8, 8)]
            if t == 1:
                src = mine
            else:
                ring[piece, chain, t - 1, part].wait_recv()
                src = buf.at[piece, part, t - 2]
                src[...] += mine[...]
            copy = pltpu.make_async_remote_copy(
                src, buf.at[piece, part, t - 1], ssem.at[piece, part, t - 1], rsem.at[piece, part, t - 1],
                device_id={"grp": lax.rem(g + sign + NG, NG)}, device_id_type=MESH,
            )
            copy.start()
            ring[piece, chain, t, part] = copy

    def image(piece):
        for part in range(2):
            ring[piece, 1, 3, part].wait_recv()
            ring[piece, 0, 4, part].wait_recv()
        lam = taucol[pl.ds(pl.multiple_of(lax.rem(me, 4) * 32 + piece * KX, 16), KX), :]
        for part in range(2):
            shift = lax.rem(128 - 32 * (2 * (g & 1) + part), 128)
            for q in range(8):
                tile = vol[piece, g, part * 8 + q] + ra[piece, part, 3, q] + rb[piece, part, 2, q]
                scale = tile[2 * KX : 3 * KX] + lam
                for c in range(2):
                    f = pltpu.roll(tile[c * KX : c * KX + KX] / scale, shift, 1)
                    hi = f.astype(BF)
                    r = c * 32 + part * KX
                    lhs[r : r + KX, q * 128 : q * 128 + 128] = hi
                    lhs[64 + r : 64 + r + KX, q * 128 : q * 128 + 128] = (f - hi.astype(F32)).astype(BF)

        def product(first):
            cols = slice(first, first + 256)
            full = jnp.dot(lhs[...], wh[:, cols], preferred_element_type=F32)
            return full[0:64] + full[64:128] + jnp.dot(lhs[0:64, :], wl[:, cols], preferred_element_type=F32)

        for n in range(4):
            c = product(n * 256)
            s = product(1024 + n * 256)
            for part in range(2):
                rows = slice(part * 32 + piece * KX, part * 32 + piece * KX + KX)
                low, high = slice(part * KX, part * KX + KX), slice(32 + part * KX, 32 + part * KX + KX)
                out[0, rows, n * 256 : n * 256 + 256] = c[low] - s[high]
                out[1, rows, n * 256 : n * 256 + 256] = s[low] + c[high]

    def owners(i, j):
        first, second = lax.rem(g + i, NG), lax.rem(g + j, NG)
        odd = first & 1
        return (first + odd * (second - first), second + odd * (first - second))

    pairs = [owners(4, 3), owners(5, 2), owners(6, 1), owners(7, 0)]

    def places(piece, first, last):
        @pl.loop(first, last)
        def _(step):
            place(piece, step)

    places(0, 0, 4)
    for step in range(4):
        send(1, step)
    places(0, 4, 6)
    for step in range(4, 6):
        send(1, step)
    places(0, 6, 8)
    for step in range(6, 8):
        send(1, step)
    spread(0, pairs[0:1])
    hop(0, 0, 1)
    hop(0, 1, 1, (1,))
    spread(0, pairs[1:2])
    hop(0, 1, 1, (0,))
    places(1, 0, 2)
    hop(0, 0, 2)
    spread(0, pairs[2:3])
    hop(0, 1, 2)
    spread(0, pairs[3:4])
    hop(0, 0, 3)
    places(1, 2, 4)
    hop(0, 1, 3)
    places(1, 4, 6)
    hop(0, 0, 4)
    places(1, 6, 8)
    spread(1, pairs[0:1])
    hop(1, 0, 1)
    hop(1, 1, 1, (1,))
    spread(1, pairs[1:2])
    hop(1, 1, 1, (0,))
    hop(1, 0, 2)
    spread(1, pairs[2:3])
    hop(1, 1, 2)
    spread(1, pairs[3:4])
    hop(1, 0, 3)
    tables()
    hop(1, 1, 3)
    image(0)
    hop(1, 0, 4)
    image(1)
    for copy in sends:
        copy.wait_send()
    for copy in ring.values():
        copy.wait_send()


def factors():
    z = np.arange(1024)
    digit = np.arange(32)[:, None]
    coarse = 2.0 * math.pi * (32 * digit * z % 1024) / 1024
    fine = 2.0 * math.pi * (digit * z % 1024) / 1024
    scale = 1.0 / 32.0
    return [np.asarray(a, np.float32) for a in (np.cos(coarse), np.sin(coarse), scale * np.cos(fine), scale * np.sin(fine))]


def on_device(spectra, ctf_sq, dest, block, pattern, pattern_table, tau):
    iota = jnp.asarray(np.tile(np.arange(256)[:, None], (1, 128)), BF)
    groups = jnp.asarray(np.tile(np.arange(128)[None, :] // 32, (128, 1)), BF)
    dma = pltpu.SemaphoreType.DMA
    small = (
        dest.reshape(1, ROWS), block.reshape(1, ROWS), pattern.reshape(1, ROWS), tau.reshape(1, 1024),
        iota, pattern_table.T, groups, *[jnp.asarray(a) for a in factors()],
    )
    operands = (spectra, ctf_sq, *small)
    image = pl.pallas_call(
        kernel,
        out_shape=jax.ShapeDtypeStruct((2, 64, 1024), F32),
        in_specs=[pl.BlockSpec(memory_space=pl.ANY)] * len(operands),
        out_specs=pl.BlockSpec(memory_space=pltpu.VMEM),
        scratch_shapes=[
            pltpu.VMEM((4, 3, ROWS, 256), BF),
            *[pltpu.VMEM(a.shape, a.dtype) for a in small],
            pltpu.VMEM((NS, 13, 16, 128), BF),
            pltpu.VMEM((NS, 12, 16, 128), BF),
            pltpu.VMEM((NS, 13, 16, 128), BF),
            pltpu.VMEM((NS, 12, 16, 128), BF),
            pltpu.VMEM((16, ROWS), F32),
            pltpu.VMEM((ROWS, ROWS), BF),
            pltpu.VMEM((16, 128), F32),
            pltpu.VMEM((COLS + 32, ROWS), BF),
            pltpu.VMEM((2, 256, ROWS), BF),
            pltpu.VMEM((4, COLS + 32, 1024), BF),
            pltpu.VMEM((NS, COLS + 32, 1024), BF),
            pltpu.VMEM((NS, COLS, 1024), BF),
            pltpu.VMEM((4, 256, 1024), BF),
            pltpu.VMEM((4, COLS, 256), F32),
            pltpu.VMEM((PIECES, NG, 16, COLS, 128), F32),
            pltpu.VMEM((PIECES, 2, 4, 8, COLS, 128), F32),
            pltpu.VMEM((PIECES, 2, 3, 8, COLS, 128), F32),
            pltpu.VMEM((1024, 2048), BF),
            pltpu.VMEM((1024, 2048), BF),
            pltpu.VMEM((128, 1024), BF),
            pltpu.VMEM((128, 128), F32),
            dma((4, 3)),
            dma((SMALL,)),
            dma((NS,)),
            dma((NS,)),
            dma((NS,)),
            dma((NS,)),
            dma((PIECES, 2, 4)),
            dma((PIECES, 2, 4)),
            dma((PIECES, 2, 3)),
            dma((PIECES, 2, 3)),
        ],
        compiler_params=pltpu.CompilerParams(
            collective_id=0, has_side_effects=True, vmem_limit_bytes=62 * 1024 * 1024
        ),
        name="backproject",
    )(*operands)
    return jnp.transpose(image.reshape(2, 2, 32, 1024), (0, 1, 3, 2))


def solution(mesh):
    rows = P(("grp", "slab"))
    wide = P(("grp", "slab"), None)
    return jax.shard_map(
        on_device,
        mesh=mesh,
        in_specs=(wide, wide, wide, rows, rows, P(), P()),
        out_specs=P(None, "grp", None, "slab"),
        check_vma=False,
    )
```

time: 122 us -> 115 us (0.943)
  the two profiles are of different devices: /device:TPU:29 before, /device:TPU:1 now
where the time goes in v3:
time: 115 us
  Pallas kernels  113 us (98%)
  local copies, waits for them, and re-layouts  1.89 us (2%)
    pallas_call x1, Pallas kernels, on_device(): pl.pallas_call(kernel, out_shape=jax.ShapeDtypeStruct((2, 64, 1024), F32)...  113 us

profile of v3, /device:TPU:1, one launch (start us, length us, event | category | flops | bytes accessed | tf_op | source)
XLA Modules:
  0.0 114.5 jit_solution(2844300927994366500)
XLA Ops:
  0.0 112.6 %backproject.1 = f32[2,64,1024]{2,1,0:T(8,128)} custom-call(bf16[512,2048]{1,0:T(8,128)(2,1)} %spec.1, bf16[512,1024]{1,0:T(8,128)(2,1)} %ctf.1, s32[1,512]{1,0:T(1,128)} %bitcast.10, s32[1,512]{1,0:T(1,128)} %bitcast.11, s32[1,512]{1,0:T(1,128)} %bitcast.12, f32[1,1024]{1,0:T(1,128)} %bitcast.9, bf16[256,128]{1,0:T(8,128)(2,1)} %constant.12.clone.rest_4_, ...), custom_call_target="tpu_custom_call" | custom-call | tf_op jit(solution)/shard_map/backproject/pallas_call | solution.py:366
  112.6 1.9 %copy.15 = f32[2,2,1024,32]{2,3,1,0:T(8,128)} copy(f32[2,2,1024,32]{2,3,1,0:T(8,128)} %bitcast.8) | data formatting | bytes 1048576

commit v4 on v3

--- a/solution.py
+++ b/solution.py
@@ -174,11 +174,14 @@
         got, rsem = ((got0, rsem0), (got1, rsem1))[piece]
         even, odd = steps_away(step)
         height = COLS + 32 if piece == 0 else COLS
+        sources = []
         for jj in range(4):
             same = 1 - lax.rem(col + jj // 2, 2)
             dx, dy = (same * e + (1 - same) * o for e, o in zip(even, odd))
             j = (lax.rem(row + dy, 4) * 4 + lax.rem(col + dx, 4)) * 2 + jj % 2
             pltpu.make_async_copy(got.at[j], got.at[j], rsem.at[j]).wait()
+            sources.append(j)
+        for jj, j in enumerate(sources):
             m = got0[j, 12].astype(F32)
             for t in range(4):
                 lanes = slice(t * 128, t * 128 + 128)

time: 115 us -> 114 us (level)
  no operation moved by 1% of the time
where the time goes in v4:
time: 114 us
  Pallas kernels  112 us (98%)
  local copies, waits for them, and re-layouts  1.89 us (2%)
    pallas_call x1, Pallas kernels, on_device(): pl.pallas_call(kernel, out_shape=jax.ShapeDtypeStruct((2, 64, 1024), F32)...  112 us

profile of v4, /device:TPU:1, one launch (start us, length us, event | category | flops | bytes accessed | tf_op | source)
XLA Modules:
  0.0 114.3 jit_solution(14759690476187642861)
XLA Ops:
  0.0 112.4 %backproject.1 = f32[2,64,1024]{2,1,0:T(8,128)} custom-call(bf16[512,2048]{1,0:T(8,128)(2,1)} %spec.1, bf16[512,1024]{1,0:T(8,128)(2,1)} %ctf.1, s32[1,512]{1,0:T(1,128)} %bitcast.10, s32[1,512]{1,0:T(1,128)} %bitcast.11, s32[1,512]{1,0:T(1,128)} %bitcast.12, f32[1,1024]{1,0:T(1,128)} %bitcast.9, bf16[256,128]{1,0:T(8,128)(2,1)} %constant.12.clone.rest_4_, ...), custom_call_target="tpu_custom_call" | custom-call | tf_op jit(solution)/shard_map/backproject/pallas_call | solution.py:369
  112.5 1.9 %copy.15 = f32[2,2,1024,32]{2,3,1,0:T(8,128)} copy(f32[2,2,1024,32]{2,3,1,0:T(8,128)} %bitcast.8) | data formatting | bytes 1048576
